TPU v7x, 32 devices: a whole 2x2x4 slice. The times are simulated.
32 devices in a mesh: prow: 2 (over core), pcol: 16 (over z, y, x).
Axes of the slice: x: 2, y: 2, z: 4, core: 2. Of those that a mesh axis runs over, the one named last changes fastest.
Arguments:
- factor_rows: float32 [8, 256, 24, 2048], P(None, 'prow', None, 'pcol'), as said below
- sensitivity: float32 [1024, 24, 2048], P('prow', None, 'pcol'), may hold values from -6 to 6
- pivots: int32 [2048], replicated, may hold values from 0 to 2047, as said below
Outputs:
- adjoint: float32 [1024, 8, 256], P(None, None, 'prow')
- updated: float32 [1024, 24, 2048], P('prow', None, 'pcol')
Inputs may be any that keep to these rules, and one draw needn't show every extreme that they name: pivots is a permutation of the first 2048 columns. `factor_rows`: in M, the entries left of each block row's diagonal block are zero and each diagonal block is lower triangular.
All inputs are finite; a program needn't handle non-finite values.
Results may differ from a plain program's by a relative error of at most 0.0001.
Values sent between devices are 32-bit elements; how exact they have to be, the bound alone decides.
No kernel may reach another device: no remote copies, remote signals or barrier semaphores. Data moves between devices by JAX's collectives and lax.ppermute only.
A program may use at most 192 MiB of HBM per device.

v0:
```python
import jax
import jax.numpy as jnp
from jax import lax
from jax.sharding import PartitionSpec as P

NB = 1024


def shards(factor_rows, sensitivity, pivots):
    pcol_count = lax.axis_size("pcol")
    row_cycles = factor_rows.shape[0]
    half_cycles = row_cycles // 2
    tile_width = factor_rows.shape[1]
    col_tiles = factor_rows.shape[2]
    local_rhs = sensitivity.shape[0]
    per_block = NB // tile_width
    pcol_index = lax.axis_index("pcol")
    tile_ids = jnp.arange(col_tiles) * pcol_count + pcol_index
    stripe_cols = pcol_count * tile_width
    gathered = lax.all_gather(sensitivity[:, :1, :], "pcol", axis=2, tiled=True)
    flat_cols = gathered.reshape(local_rhs, stripe_cols)
    swapped = jnp.take(flat_cols, pivots, axis=1)
    merged = swapped.reshape(local_rhs, 1, pcol_count, tile_width)
    own_tiles = lax.dynamic_index_in_dim(merged, pcol_index, 2, keepdims=False)
    working = jnp.concatenate([own_tiles, sensitivity[:, 1:, :]], axis=1)

    def tile_range(section):
        return (
            section * per_block // pcol_count,
            ((section + 1) * per_block - 1) // pcol_count + 1,
        )

    def solve_block(working, section):
        low_tile, high_tile = tile_range(section)
        chosen = tile_ids[low_tile:high_tile]
        inside = ((chosen >= section * per_block) & (chosen < (section + 1) * per_block)).astype(
            jnp.float32
        )
        masked = working[:, low_tile:high_tile, :] * inside[None, :, None]
        all_rhs = lax.all_gather(masked, "prow", axis=0, tiled=True)
        inverse_tiles = factor_rows[
            section * half_cycles : (section + 1) * half_cycles, :, low_tile:high_tile, :
        ]
        partial_sum = jnp.einsum(
            "hbu,atbu->hat",
            all_rhs,
            inverse_tiles,
            precision=lax.Precision.HIGHEST,
            preferred_element_type=jnp.float32,
        )
        partial_sum = partial_sum.reshape(all_rhs.shape[0], half_cycles * tile_width)
        return lax.psum(partial_sum, "pcol")

    solved_first = solve_block(working, 0)
    low_tile, high_tile = tile_range(1)
    next_tiles = high_tile - low_tile
    first_rows = factor_rows[:half_cycles, :, low_tile:high_tile, :].reshape(
        half_cycles * tile_width, next_tiles * tile_width
    )
    picked = solved_first
    early = lax.psum_scatter(
        jnp.dot(
            picked, first_rows, precision=lax.Precision.HIGHEST, preferred_element_type=jnp.float32
        ),
        "prow",
        scatter_dimension=0,
        tiled=True,
    ).reshape(local_rhs, next_tiles, tile_width)
    chosen = tile_ids[low_tile:high_tile]
    inside = ((chosen >= per_block) & (chosen < 2 * per_block)).astype(jnp.float32)
    working = working.at[:, low_tile:high_tile, :].add(-early * inside[None, :, None])
    solved_second = solve_block(working, 1)
    both_solved = jnp.concatenate([solved_first, solved_second], axis=1)
    all_rows = factor_rows.reshape(row_cycles * tile_width, col_tiles * tile_width)
    picked = both_solved
    change = lax.psum_scatter(
        jnp.dot(
            picked, all_rows, precision=lax.Precision.HIGHEST, preferred_element_type=jnp.float32
        ),
        "prow",
        scatter_dimension=0,
        tiled=True,
    ).reshape(local_rhs, col_tiles, tile_width)
    keep_cols = (tile_ids >= 2 * per_block).astype(jnp.float32)
    working = working - change * keep_cols[None, :, None]
    adjoint = jnp.concatenate([solved_first, solved_second], axis=1).reshape(
        solved_first.shape[0], row_cycles, tile_width
    )
    return (adjoint, working)


def solution(mesh):
    return jax.shard_map(
        shards,
        mesh=mesh,
        in_specs=(P(None, "prow", None, "pcol"), P("prow", None, "pcol"), P()),
        out_specs=(P(None, None, "prow"), P("prow", None, "pcol")),
        check_vma=False,
    )
```

profile of v0, /device:TPU:0, one launch (start us, length us, event | category | flops | bytes accessed | tf_op | source)
XLA Modules:
  0.0 478.7 jit_solution(9994754397476234976)
XLA Ops:
  7.2 0.0 all-gather.3.cloned.1.call-start
  7.2 1.7 slice.41
  8.9 0.8 copy.11
  9.8 0.0 all-gather.3.cloned.1.call-update
  9.8 0.0 all-reduce.3.cloned.1.call-start
  9.9 0.7 and_bitcast_fusion
  10.7 0.7 fusion.4
  11.4 2.5 fusion.5
  13.9 76.2 %all-gather.3.cloned.1.call-done = f32[512,1,2048]{0,2,1:T(8,128)} async-done(((f32[512,1,128]{0,2,1:T(8,128)}), f32[512,1,2048]{0,2,1:T(8,128)}) %all-gather.3.cloned.1.call-update) | async-done | bytes 4194320 | tf_op jit(solution)/shard_map/all_gather | solution.py:20
  90.2 11.7 %gather_fusion = f32[2048,512]{1,0:T(8,128)} fusion(f32[512,2048]{0,1:T(8,128)} %bitcast.40, s32[2048]{0:T(1024)S(1)} %fusion.4), kind=kCustom, calls=%fused_computation | custom fusion | bytes 8396800 | tf_op jit(solution)/shard_map/jit(_take)/gather | solution.py:22
  101.8 1.0 constant_dynamic-slice_fusion.1
  102.8 0.1 copy.12
  103.0 2.2 all_gather.10
  105.2 3.1 fusion.6
  108.3 0.0 all-reduce.3.cloned.1.call-update
  108.3 0.0 reduce-scatter.3.cloned.1.call-start
  108.4 124.7 %all-reduce.3.cloned.1.call-done = f32[1024,512]{1,0:T(8,128)} async-done(((f32[1024,512]{1,0:T(8,128)}), f32[1024,512]{1,0:T(8,128)}) %all-reduce.3.cloned.1.call-update) | async-done | bytes 2097168 | tf_op jit(solution)/shard_map/psum | solution.py:52
  233.0 4.2 fusion.7
  237.2 0.0 copy-start
  237.2 0.0 reduce-scatter.3.cloned.1.call-update
  237.2 0.0 all-reduce.5.cloned.1.call-start
  237.4 7.3 %reduce-scatter.3.cloned.1.call-done = f32[512,128]{1,0:T(8,128)} async-done(((f32[1024,128]{1,0:T(8,128)}), f32[512,128]{1,0:T(8,128)}) %reduce-scatter.3.cloned.1.call-update) | async-done | bytes 262160 | tf_op jit(solution)/shard_map/reduce_scatter | solution.py:61
  244.7 1.0 broadcast_multiply_fusion
  245.7 2.2 all-gather
  247.9 3.1 fusion.8
  251.0 0.0 all-reduce.5.cloned.1.call-update
  251.0 0.2 reduce-scatter.5.cloned.1.call-start
  251.2 0.0 copy-done
  251.2 1.6 constant_dynamic-update-slice_fusion.1
  252.8 125.4 %all-reduce.5.cloned.1.call-done = f32[1024,512]{1,0:T(8,128)} async-done(((f32[1024,512]{1,0:T(8,128)}), f32[1024,512]{1,0:T(8,128)}) %all-reduce.5.cloned.1.call-update) | async-done | bytes 2097168 | tf_op jit(solution)/shard_map/psum | solution.py:52
  378.3 3.2 constant_dynamic-update-slice_fusion
  381.4 60.8 %fusion = f32[1024,3072]{1,0:T(8,128)} fusion(f32[1024,1024]{1,0:T(8,128)} %constant_dynamic-update-slice_fusion, f32[128,8,24,128]{3,2,1,0:T(8,128)} %bitcast.55), kind=kOutput, calls=%fused_computation.1 | convolution fusion | flops 38654705664 | bytes 29360128 | tf_op jit(solution)/shard_map/dot_general | solution.py:77
  442.2 0.0 reduce-scatter.5.cloned.1.call-update
  442.2 3.4 slice.45
  445.6 4.0 pad_maximum_fusion
  449.6 8.2 %scatter-add.4 = f32[512,24,128]{2,1,0:T(8,128)} dynamic-update-slice(f32[512,24,128]{2,1,0:T(8,128)} %pad_maximum_fusion, f32[512,1,128]{2,1,0:T(1,128)S(1)} %bitcast.52, s32[]{:T(128)} %constant.48.clone.1, s32[]{:T(128)} %constant.48.clone.1, s32[]{:T(128)} %constant.48.clone.1) | dynamic-update-slice | bytes 524292 | tf_op jit(solution)/shard_map/scatter-add | solution.py:71
  457.8 6.1 %copy.13 = f32[128,8,8,128]{3,2,1,0:T(8,128)} copy(f32[128,8,8,128]{3,1,2,0:T(8,128)} %bitcast.43) | data formatting | bytes 8388608
  464.0 0.0 reduce-scatter.5.cloned.1.call-done
  464.0 0.0 slice-start
  464.0 0.0 slice-start.1
  464.0 4.3 copy.15
  468.3 0.0 slice-done
  468.3 0.3 slice-done.1
  468.6 3.6 fusion.3
  (6 shorter events, 0.1 us)
Async XLA Ops:
  7.2 83.0 %all-gather.3.cloned.1.call-start = ((), (), s32[]{:S(2)}) async-start(), calls=%async_computation.2 | async-start | bytes 4456448 | tf_op jit(solution)/shard_map/all_gather | solution.py:20
  9.8 223.2 %all-reduce.3.cloned.1.call-start = ((), (), s32[]{:S(2)}) async-start(), calls=%async_computation.3 | async-start | bytes 4194304 | tf_op jit(solution)/shard_map/psum | solution.py:52
  108.3 136.4 %reduce-scatter.3.cloned.1.call-start = ((), (), s32[]{:S(2)}) async-start(), calls=%async_computation.4 | async-start | bytes 786432 | tf_op jit(solution)/shard_map/reduce_scatter | solution.py:61
  237.2 14.0 %copy-start = (f32[1024,512]{1,0:T(8,128)S(1)}, f32[1024,512]{1,0:T(8,128)}, u32[]{:S(2)}) copy-start(f32[1024,512]{1,0:T(8,128)} %all-reduce.3.cloned.1.call-done) | copy-start | bytes 6291460
  237.2 141.0 %all-reduce.5.cloned.1.call-start = ((), (), s32[]{:S(2)}) async-start(), calls=%async_computation.5 | async-start | bytes 4194304 | tf_op jit(solution)/shard_map/psum | solution.py:52
  251.0 213.0 %reduce-scatter.5.cloned.1.call-start = ((), (), s32[]{:S(2)}) async-start(), calls=%async_computation.6 | async-start | bytes 18874368 | tf_op jit(solution)/shard_map/reduce_scatter | solution.py:76
  464.0 4.4 slice-start
  464.0 4.7 slice-start.1
Sparse Core Ops, SparseCore 0:
  11.3 78.7 all-gather.2
  108.4 124.5 all-reduce.2
  237.4 7.2 reduce-scatter.2
  251.1 127.1 all-reduce.4
  442.4 20.8 reduce-scatter.4
where the time goes:
time: 479 us
  waiting for transfers between devices  334 us (70%)
  matrix products  71.2 us (15%)
  local copies, waits for them, and re-layouts  45.1 us (9%)
  between operations  14 us (3%)
  other arithmetic  9.97 us (2%)
    psum x2, waiting for transfers between devices, solve_block(): return lax.psum(partial_sum, 'pcol')  250 us
    all_gather x1, waiting for transfers between devices, shards(): gathered = lax.all_gather(sensitivity[:, :1, :], 'pcol', axis=2, tiled=True)  76.2 us
    dot_general x1, matrix products, shards(): jnp.dot(picked, all_rows, precision=lax.Precision.HIGHEST, preferred_elem...  60.8 us
    unnamed x11, local copies, waits for them, and re-layouts  13.4 us
    gather x1, local copies, waits for them, and re-layouts, shards(): swapped = jnp.take(flat_cols, pivots, axis=1)  11.7 us
  transfers between devices with their start and end apart: 5, of which 4 were waited for; matrix products, arithmetic and copies ran while one was open for 6% of the time, Pallas kernels for 0%

commit v1 on v0

--- a/solution.py
+++ b/solution.py
@@ -49,7 +49,7 @@
             preferred_element_type=jnp.float32,
         )
         partial_sum = partial_sum.reshape(all_rhs.shape[0], half_cycles * tile_width)
-        return lax.psum(partial_sum, "pcol")
+        return jnp.sum(lax.all_gather(partial_sum, "pcol"), axis=0)
 
     solved_first = solve_block(working, 0)
     low_tile, high_tile = tile_range(1)

time: 479 us -> 951 us (1.99)
  waiting for transfers between devices: 334 us -> 784 us
  other arithmetic: 9.97 us -> 38.9 us
    all_gather x0 -> x2, waiting for transfers between devices: none -> 702 us  [solve_block(): return jnp.sum(lax.all_gather(partial_sum, 'pcol'), axis=0)]
    psum x2 -> x0, waiting for transfers between devices: 250 us -> none  [solve_block(): return lax.psum(partial_sum, 'pcol')]
    reduce_sum x0 -> x2, other arithmetic: none -> 26.8 us  [solve_block(): return jnp.sum(lax.all_gather(partial_sum, 'pcol'), axis=0)]
  transfers between devices with their start and end apart: 5 -> 5, of which waited for: 4 -> 4; matrix products, arithmetic and copies ran while one was open for 6% -> 3% of each run, Pallas kernels for 0% -> 0%
where the time goes in v1:
time: 951 us; the launch traced here: 950 us
  waiting for transfers between devices  784 us (82%)
  matrix products  71.4 us (8%)
  other arithmetic  38.9 us (4%)
  local copies, waits for them, and re-layouts  37.2 us (4%)
  between operations  14 us (1%)
    all_gather x2, waiting for transfers between devices, solve_block(): return jnp.sum(lax.all_gather(partial_sum, 'pcol'), axis=0)  702 us
    all_gather x1, waiting for transfers between devices, shards(): gathered = lax.all_gather(sensitivity[:, :1, :], 'pcol', axis=2, tiled=True)  76.2 us
    dot_general x1, matrix products, shards(): jnp.dot(picked, all_rows, precision=lax.Precision.HIGHEST, preferred_elem...  62.6 us
    reduce_sum x2, other arithmetic, solve_block(): return jnp.sum(lax.all_gather(partial_sum, 'pcol'), axis=0)  26.8 us
  transfers between devices with their start and end apart: 5, of which 4 were waited for; matrix products, arithmetic and copies ran while one was open for 3% of the time, Pallas kernels for 0%

profile of v1, /device:TPU:0, one launch (start us, length us, event | category | flops | bytes accessed | tf_op | source)
XLA Modules:
  0.0 950.2 jit_solution(9593303263309133836)
XLA Ops:
  7.2 0.0 all-gather.7.cloned.1.call-start
  7.2 1.7 slice.41
  8.9 0.8 copy.11
  9.8 0.0 all-gather.7.cloned.1.call-update
  9.8 0.0 all-gather.9.cloned.1.call-start
  9.9 0.7 and_bitcast_fusion
  10.7 0.7 fusion.5
  11.4 2.5 fusion.7
  13.9 76.2 %all-gather.7.cloned.1.call-done = f32[512,1,2048]{0,2,1:T(8,128)} async-done(((f32[512,1,128]{0,2,1:T(8,128)}), f32[512,1,2048]{0,2,1:T(8,128)}) %all-gather.7.cloned.1.call-update) | async-done | bytes 4194320 | tf_op jit(solution)/shard_map/all_gather | solution.py:20
  90.2 11.7 %gather_fusion = f32[2048,512]{1,0:T(8,128)} fusion(f32[512,2048]{0,1:T(8,128)} %bitcast.42, s32[2048]{0:T(1024)S(1)} %fusion.5), kind=kCustom, calls=%fused_computation | custom fusion | bytes 8396800 | tf_op jit(solution)/shard_map/jit(_take)/gather | solution.py:22
  101.8 1.0 constant_dynamic-slice_fusion.1
  102.8 0.1 copy.12
  103.0 2.2 all_gather.16
  105.2 3.1 fusion.8
  108.3 0.0 all-gather.9.cloned.1.call-update
  108.3 0.0 reduce-scatter.3.cloned.1.call-start
  108.4 349.6 %all-gather.9.cloned.1.call-done = f32[16384,512]{1,0:T(8,128)} async-done(((f32[1024,512]{1,0:T(8,128)}), f32[16384,512]{1,0:T(8,128)}) %all-gather.9.cloned.1.call-update) | async-done | bytes 33554448 | tf_op jit(solution)/shard_map/all_gather | solution.py:52
  457.9 12.7 %reduce_sum.18 = f32[1024,512]{1,0:T(8,128)S(1)} reduce(f32[16,1024,512]{2,1,0:T(8,128)} %bitcast.44, f32[]{:T(128)} %constant.57.clone.1), dimensions={0}, to_apply=%region_0.1 | reduce | flops 7864320 | bytes 35651588 | tf_op jit(solution)/shard_map/reduce_sum | solution.py:52
  470.7 2.6 fusion.9
  473.3 0.0 reduce-scatter.3.cloned.1.call-update
  473.3 0.0 all-gather.11.cloned.1.call-start
  473.4 6.2 reduce-scatter.3.cloned.1.call-done
  479.6 1.0 broadcast_multiply_fusion
  480.6 2.2 all-gather.1
  482.8 3.1 fusion.10
  485.9 0.0 all-gather.11.cloned.1.call-update
  485.9 0.2 reduce-scatter.5.cloned.1.call-start
  486.1 351.9 %all-gather.11.cloned.1.call-done = f32[16384,512]{1,0:T(8,128)} async-done(((f32[1024,512]{1,0:T(8,128)}), f32[16384,512]{1,0:T(8,128)}) %all-gather.11.cloned.1.call-update) | async-done | bytes 33554448 | tf_op jit(solution)/shard_map/all_gather | solution.py:52
  838.1 14.0 %reduce_sum.19 = f32[1024,512]{1,0:T(8,128)} reduce(f32[16,1024,512]{2,1,0:T(8,128)} %bitcast.43, f32[]{:T(128)} %constant.57.clone.1), dimensions={0}, to_apply=%region_2.3 | reduce | flops 7864320 | bytes 35651588 | tf_op jit(solution)/shard_map/reduce_sum | solution.py:52
  852.1 62.6 %fusion = f32[1024,3072]{1,0:T(8,128)} fusion(f32[128,8,24,128]{3,2,1,0:T(8,128)} %bitcast.58, f32[1024,512]{1,0:T(8,128)} %reduce_sum.19, f32[1024,512]{1,0:T(8,128)S(1)} %reduce_sum.18), kind=kOutput, calls=%fused_computation.1 | convolution fusion | flops 38655754240 | bytes 29360128 | tf_op jit(solution)/shard_map/dot_general | solution.py:77
  914.7 0.0 reduce-scatter.5.cloned.1.call-update
  914.7 3.4 slice.45
  918.1 3.5 pad_maximum_fusion
  921.6 8.3 scatter-add.4
  929.8 2.6 fusion.4
  932.5 3.0 copy.13
  935.5 0.0 reduce-scatter.5.cloned.1.call-done
  935.5 0.0 slice-start
  935.5 0.0 slice-start.1
  935.5 4.3 copy.15
  939.8 0.0 slice-done
  939.8 0.3 slice-done.1
  940.2 3.6 fusion.3
  (6 shorter events, 0.1 us)
Async XLA Ops:
  7.2 83.0 %all-gather.7.cloned.1.call-start = ((), (), s32[]{:S(2)}) async-start(), calls=%async_computation.2 | async-start | bytes 4456448 | tf_op jit(solution)/shard_map/all_gather | solution.py:20
  9.8 448.1 %all-gather.9.cloned.1.call-start = ((), (), s32[]{:S(2)}) async-start(), calls=%async_computation.5 | async-start | bytes 35651584 | tf_op jit(solution)/shard_map/all_gather | solution.py:52
  108.3 371.3 %reduce-scatter.3.cloned.1.call-start = ((), (), s32[]{:S(2)}) async-start(), calls=%async_computation.3 | async-start | bytes 786432 | tf_op jit(solution)/shard_map/reduce_scatter | solution.py:61
  473.3 364.8 %all-gather.11.cloned.1.call-start = ((), (), s32[]{:S(2)}) async-start(), calls=%async_computation.6 | async-start | bytes 35651584 | tf_op jit(solution)/shard_map/all_gather | solution.py:52
  485.9 449.6 %reduce-scatter.5.cloned.1.call-start = ((), (), s32[]{:S(2)}) async-start(), calls=%async_computation.4 | async-start | bytes 18874368 | tf_op jit(solution)/shard_map/reduce_scatter | solution.py:76
  935.5 4.4 slice-start
  935.5 4.7 slice-start.1
Sparse Core Ops, SparseCore 0:
  11.3 78.7 all-gather.6
  108.4 349.4 all-gather.8
  473.4 6.1 reduce-scatter.2
  486.0 352.0 all-gather.10
  914.8 19.6 reduce-scatter.4
